TPU v7x, 512 devices: a whole 4x8x8 slice. The times are simulated.
512 devices in a mesh: seq: 64 (over x, y, core), chan: 8 (over z).
Axes of the slice: x: 4, y: 8, z: 8, core: 2. Of those that a mesh axis runs over, the one named last changes fastest.
Arguments:
- gate_outer: bfloat16 [8192, 4096], P('seq', 'chan'), may hold values from -520 to 520
- gate_inner: bfloat16 [8192, 4096], P('seq', 'chan'), may hold values from -6 to 6
- value_in: bfloat16 [8192, 4096], P('seq', 'chan'), may hold values from -6 to 6
- pole_rates: float32 [8, 4096], P(None, 'chan'), may hold values from 0 to 1, as said below
- pole_weights: float32 [8, 4096], P(None, 'chan'), may hold values from -4 to 4
- skip_gain: float32 [4096], P('chan'), may hold values from -1 to 1
- query_rows: bfloat16 [8192, 4096], P('seq', 'chan'), may hold values from -6 to 6
- key_rows: bfloat16 [8192, 4096], P('seq', 'chan'), may hold values from -6 to 6
Outputs:
- mixed: bfloat16 [8192, 4096], P('seq', 'chan')
Inputs may be any that keep to these rules, and one draw needn't show every extreme that they name: `pole_rates`: each rate is positive and at most 1/30.
All inputs are finite; a program needn't handle non-finite values.
Results may differ from a plain program's by a relative error of at most 0.0065.
Values may be sent and summed in bfloat16 or wider, within the bound.
A program may use at most 128 MiB of HBM per device.

v0:
```python
import math

import jax
import jax.numpy as jnp
from jax import lax
from jax.sharding import PartitionSpec as P

HD = 128


def prefix(part, axis, combine, identity):
    place = lax.axis_index(axis)
    gathered = jax.tree.map(lambda a: lax.all_gather(a, axis), part)
    state = jax.tree.map(lambda a, e: jnp.zeros_like(a) + jnp.asarray(e, a.dtype), part, identity)

    def one(turn, state):
        return combine(
            state, jax.tree.map(lambda a: lax.dynamic_index_in_dim(a, turn, 0, False), gathered)
        )

    return lax.fori_loop(0, place, one, state)


def block_update(carried, queries, query_pos, key_part, value_part, key_start, score_scale):
    run_max, run_sum, run_acc = carried
    heads_here = run_max.shape[0]
    key_count = key_part.shape[0]
    query_heads = queries.reshape(queries.shape[0], heads_here, -1)
    key_heads = key_part.reshape(key_count, heads_here, -1)
    value_heads = value_part.reshape(key_count, heads_here, -1)
    scores = (
        jnp.einsum("qhd,khd->hqk", query_heads, key_heads, preferred_element_type=jnp.float32)
        * score_scale
    )
    key_pos = key_start + jnp.arange(key_count, dtype=jnp.int32)
    visible = key_pos[None, None, :] <= query_pos[None, :, None]
    scores = jnp.where(visible, scores, -1e30)
    new_max = jnp.maximum(run_max, jnp.max(scores, axis=2))
    rescale = jnp.exp(run_max - new_max)
    expo = jnp.where(visible, jnp.exp(scores - new_max[:, :, None]), 0.0)
    new_sum = run_sum * rescale + jnp.sum(expo, axis=2)
    new_acc = run_acc * rescale[:, :, None] + jnp.einsum(
        "hqk,khd->hqd", expo.astype(jnp.bfloat16), value_heads, preferred_element_type=jnp.float32
    )
    return (new_max, new_sum, new_acc)


def fold_keys(carried, queries, query_pos, pieces, score_scale):
    key_piece, value_piece = pieces
    count_rows = key_piece.shape[0]
    step_rows = math.gcd(count_rows, 1024)

    def one_step(step_index, current):
        sub_start = step_index * step_rows
        key_part = lax.dynamic_slice_in_dim(key_piece, sub_start, step_rows, 0)
        value_part = lax.dynamic_slice_in_dim(value_piece, sub_start, step_rows, 0)
        return block_update(
            current, queries, query_pos, key_part, value_part, sub_start, score_scale
        )

    return lax.fori_loop(0, count_rows // step_rows, one_step, carried)


def finish(carried):
    run_max, run_sum, run_acc = carried
    normed = run_acc / run_sum[:, :, None]
    heads_here, rows_here, depth = normed.shape
    return (
        jnp.transpose(normed, (1, 0, 2)).reshape(rows_here, heads_here * depth).astype(jnp.bfloat16)
    )


def local(
    gate_outer, gate_inner, value_in, pole_rates, pole_weights, skip_gain, query_rows, key_rows
):
    tok_rows, width = gate_outer.shape
    poles_here = pole_rates.shape[0]
    seq_index = lax.axis_index("seq")
    chan_count = lax.axis_size("chan")
    gated = gate_inner.astype(jnp.float32) * value_in.astype(jnp.float32)
    offsets = jnp.arange(tok_rows, dtype=jnp.float32)
    growth = jnp.exp(offsets[:, None, None] * pole_rates[None, :, :])
    weighted = growth * gated[:, None, :]
    lower = (jnp.arange(tok_rows)[:, None] >= jnp.arange(tok_rows)[None, :]).astype(jnp.float32)
    running = jnp.dot(
        lower, weighted.reshape(tok_rows, poles_here * width), precision=lax.Precision.HIGHEST
    )
    running = running.reshape(tok_rows, poles_here, width)
    block_span = jnp.float32(tok_rows)
    summary = running[-1] * jnp.exp(-(block_span - 1.0) * pole_rates)

    def chain_states(earlier, later):
        fade = jnp.exp(-block_span * later[1] * pole_rates)
        return (later[0] + fade * earlier[0], earlier[1] + later[1])

    identity = (jnp.zeros_like(summary), jnp.zeros((1, 1), jnp.float32))
    carry_in, block_count = prefix(
        (summary, jnp.ones((1, 1), jnp.float32)), "seq", chain_states, identity
    )
    decayed = jnp.exp(-offsets[:, None, None] * pole_rates[None, :, :])
    modal = decayed * (running + (jnp.exp(-pole_rates) * carry_in)[None, :, :])
    filtered = jnp.sum(modal * (pole_weights * jnp.sqrt(pole_rates))[None, :, :], axis=1)
    conv_out = gate_outer.astype(jnp.float32) * (filtered + skip_gain[None, :] * gated)
    local_squares = jnp.sum(conv_out * conv_out, axis=1)
    total_squares = lax.psum(local_squares, "chan")
    mean_square = total_squares / (width * chan_count)
    values = (conv_out * lax.rsqrt(mean_square[:, None] + 1e-06)).astype(jnp.bfloat16)
    score_scale = HD ** (-0.5)
    heads_here = width // HD
    my_start = seq_index * tok_rows
    all_pos = my_start + jnp.arange(tok_rows, dtype=jnp.int32)
    final_state = fold_keys(
        (
            jnp.full((heads_here, tok_rows), -1e30, jnp.float32),
            jnp.zeros((heads_here, tok_rows), jnp.float32),
            jnp.zeros((heads_here, tok_rows, HD), jnp.float32),
        ),
        query_rows,
        all_pos,
        (
            lax.all_gather(key_rows, "seq", axis=0, tiled=True),
            lax.all_gather(values, "seq", axis=0, tiled=True),
        ),
        score_scale,
    )
    mixed = finish(final_state)
    return mixed


def solution(mesh):
    in_specs = (
        P("seq", "chan"),
        P("seq", "chan"),
        P("seq", "chan"),
        P(None, "chan"),
        P(None, "chan"),
        P("chan"),
        P("seq", "chan"),
        P("seq", "chan"),
    )
    out_specs = P("seq", "chan")
    return jax.shard_map(local, mesh=mesh, in_specs=in_specs, out_specs=out_specs, check_vma=False)
```

profile of v0, /device:TPU:1, one launch (start us, length us, event | category | flops | bytes accessed | tf_op | source)
XLA Modules:
  0.0 426.7 jit_solution(17308309685470993890)
XLA Ops:
  7.3 1.0 convert_multiply_fusion
  8.5 1.6 copy.36
  10.2 1.6 fusion.21
  13.4 3.0 copy.37
  16.4 1.3 dynamic-slice
  18.5 130.3 %all-reduce = f32[64]{0:T(128)S(1)} all-reduce(f32[64]{0:T(128)S(1)} %dynamic-update-slice), channel_id=1, replica_groups=mesh['seq'=64,'chan'=8] {'seq'}, use_global_device_ids=true, to_apply=%add | all-reduce | flops 64 | bytes 512
  148.8 2.0 while.30
  149.5 1.4 bitcast_add_fusion.3
  150.9 2.6 fusion.20
  153.7 16.0 %psum.7 = f32[128]{0:T(128)S(1)} all-reduce(f32[128]{0:T(128)S(1)} %multiply_reduce_fusion), channel_id=1, replica_groups=mesh['seq'=64,'chan'=8] {'chan'}, use_global_device_ids=true, to_apply=%region_4.5 | all-reduce | flops 128 | bytes 1024 | tf_op jit(solution)/shard_map/psum | solution.py:105
  170.5 21.5 %all-gather.5.cloned.1.call-done = bf16[8192,512]{0,1:T(8,128)(2,1)} async-done(((bf16[128,512]{0,1:T(8,128)(2,1)}), bf16[8192,512]{0,1:T(8,128)(2,1)}) %all-gather.5.cloned.1.call-update) | async-done | bytes 8388624 | tf_op jit(solution)/shard_map/all_gather | solution.py:121
  192.0 183.1 %all-gather.7.cloned.1.call-done = bf16[8192,512]{1,0:T(8,128)(2,1)} async-done(((bf16[128,512]{1,0:T(8,128)(2,1)}), bf16[8192,512]{1,0:T(8,128)(2,1)}) %all-gather.7.cloned.1.call-update) | async-done | bytes 8388624 | tf_op jit(solution)/shard_map/all_gather | solution.py:122
  375.1 44.3 %while.31 = (s32[]{:T(128)}, f32[4,128]{1,0:T(4,128)S(1)}, f32[4,128]{1,0:T(4,128)S(1)}, f32[4,128,128]{2,1,0:T(8,128)S(1)}, bf16[8192,512]{0,1:T(8,128)(2,1)}, ...) while((s32[]{:T(128)}, f32[4,128]{1,0:T(4,128)S(1)}, ...), condition=%wide.region_8.9_spmd.clone, body=%wide.region_5.8_spmd.clone.sunk | while | flops 275582592 | bytes 15901895 | solution.py:61
  375.3 1.3 constant_dynamic-slice_fusion.6
  377.2 1.3 constant_dynamic-slice_fusion.5
  380.9 1.3 constant_dynamic-slice_fusion.6
  382.7 1.3 constant_dynamic-slice_fusion.5
  385.2 0.9 convolution_add_fusion.2
  386.4 1.3 constant_dynamic-slice_fusion.6
  388.2 1.3 constant_dynamic-slice_fusion.5
  391.9 1.3 constant_dynamic-slice_fusion.6
  393.8 1.3 constant_dynamic-slice_fusion.5
  396.3 0.9 convolution_add_fusion.2
  397.5 1.3 constant_dynamic-slice_fusion.6
  399.3 1.3 constant_dynamic-slice_fusion.5
  403.0 1.3 constant_dynamic-slice_fusion.6
  404.9 1.3 constant_dynamic-slice_fusion.5
  407.4 0.9 convolution_add_fusion.2
  408.5 1.3 constant_dynamic-slice_fusion.6
  410.4 1.3 constant_dynamic-slice_fusion.5
  414.1 1.3 constant_dynamic-slice_fusion.6
  415.9 1.3 constant_dynamic-slice_fusion.5
  (119 shorter events, 25.8 us)
Async XLA Ops:
  6.5 142.3 %all-gather.9.cloned.1.call-start = ((), (), s32[]{:S(2)}) async-start(), calls=%async_computation.2 | async-start | bytes 1064960 | tf_op jit(solution)/shard_map/all_gather | solution.py:13
  10.2 1.7 copy-start.1
  10.2 2.3 copy-start.5
  12.5 179.6 %all-gather.5.cloned.1.call-start = ((), (), s32[]{:S(2)}) async-start(), calls=%async_computation | async-start | bytes 8519680 | tf_op jit(solution)/shard_map/all_gather | solution.py:121
  13.3 361.8 %all-gather.7.cloned.1.call-start = ((), (), s32[]{:S(2)}) async-start(), calls=%async_computation.1 | async-start | bytes 8519680 | tf_op jit(solution)/shard_map/all_gather | solution.py:122
  13.4 137.5 %copy-start.6 = (f32[8,512]{1,0:T(8,128)S(1)}, f32[8,512]{1,0:T(8,128)}, u32[]{:S(2)}) copy-start(f32[8,512]{1,0:T(8,128)} %param.16) | copy-start | bytes 49156
  16.4 137.1 %copy-start.2 = (bf16[128,512]{1,0:T(8,128)(2,1)S(1)}, bf16[128,512]{1,0:T(8,128)(2,1)}, u32[]{:S(2)}) copy-start(bf16[128,512]{1,0:T(8,128)(2,1)} %param.14) | copy-start | bytes 393220
  16.4 137.1 %copy-start.3 = (bf16[128,512]{1,0:T(8,128)(2,1)S(1)}, bf16[128,512]{1,0:T(8,128)(2,1)}, u32[]{:S(2)}) copy-start(bf16[128,512]{1,0:T(8,128)(2,1)} %param.13) | copy-start | bytes 393220
  16.4 137.1 %copy-start.4 = (bf16[128,512]{1,0:T(8,128)(2,1)S(1)}, bf16[128,512]{1,0:T(8,128)(2,1)}, u32[]{:S(2)}) copy-start(bf16[128,512]{1,0:T(8,128)(2,1)} %param.12) | copy-start | bytes 393220
  16.4 137.1 %copy-start.7 = (f32[512]{0:T(512)S(1)}, f32[512]{0:T(512)}, u32[]{:S(2)}) copy-start(f32[512]{0:T(512)} %param.17) | copy-start | bytes 6148
  150.9 224.2 %copy-start = (bf16[128,512]{1,0:T(8,128)(2,1)S(1)}, bf16[128,512]{1,0:T(8,128)(2,1)}, u32[]{:S(2)}) copy-start(bf16[128,512]{1,0:T(8,128)(2,1)} %param.18) | copy-start | bytes 393220
Sparse Core Ops, SparseCore 0:
  12.6 87.8 all-gather.8
  103.6 88.3 all-gather.4
  195.4 179.6 all-gather.6
where the time goes:
time: 433 us; the launch traced here: 427 us
  waiting for transfers between devices  205 us (47%)
  blocking collectives  146 us (34%)
  local copies, waits for them, and re-layouts  33.7 us (8%)
  other arithmetic  14.1 us (3%)
  matrix products  13.9 us (3%)
  between operations  13.3 us (3%)
    all_gather x1, waiting for transfers between devices, local(): lax.all_gather(values, 'seq', axis=0, tiled=True)  183 us
    unnamed x1, blocking collectives  130 us
    all_gather x1, waiting for transfers between devices, local(): lax.all_gather(key_rows, 'seq', axis=0, tiled=True)  21.5 us
    psum x1, blocking collectives, local(): total_squares = lax.psum(local_squares, 'chan')  16 us
    dynamic_slice x16, local copies, waits for them, and re-layouts, one_step(): value_part = lax.dynamic_slice_in_dim(value_piece, sub_start, step_rows, 0)  14.7 us
    dynamic_slice x8, local copies, waits for them, and re-layouts, one_step(): key_part = lax.dynamic_slice_in_dim(key_piece, sub_start, step_rows, 0)  10.4 us
  transfers between devices with their start and end apart: 3, of which 2 were waited for; matrix products, arithmetic and copies ran while one was open for 3% of the time, Pallas kernels for 0%

commit v1 on v0

v1 whole, which is shorter than its diff:
```python
import functools
import math

import jax
import jax.numpy as jnp
from jax import lax
from jax.experimental import pallas as pl
from jax.experimental.pallas import tpu as pltpu
from jax.sharding import PartitionSpec as P

HD = 128
CORES = 2
SUB = 32
MESH = pl.DeviceIdType.MESH
NEG = -1e30


def kernel(
    X,
    Y,
    Z,
    go_hbm,
    gi_hbm,
    vi_hbm,
    pr_ref,
    pw_ref,
    sg_ref,
    q_hbm,
    k_hbm,
    o_ref,
    go,
    gi,
    vi,
    g,
    y0,
    cv,
    ct,
    dd,
    fp,
    e_own,
    e_sib,
    tb,
    rb,
    sq,
    vs,
    qb,
    kb,
    vb,
    pt,
    ms,
    ls,
    ac,
    orx,
    fs,
    s_in,
    s_e,
    s_t,
    s_r,
    s_s,
    s_q,
    s_kx,
    s_k,
    s_vx,
    s_v,
    s_m,
    s_o,
):
    T = go.shape[0]
    W = go.shape[1]
    D = Y // 2
    SPAN = float(CORES * T)
    s = lax.axis_index("seq")
    z = lax.axis_index("chan")
    c = lax.rem(s, CORES)
    chip = s // CORES
    y = lax.rem(chip, Y)
    x = chip // Y

    def seq_id(xx, yy, cc):
        return {"seq": (xx * Y + yy) * CORES + cc}

    sib = {"seq": s + 1 - 2 * c}
    peers = [sib]
    peers += [seq_id(x, lax.rem(y + k, Y), c) for k in range(1, Y)]
    peers += [seq_id(lax.rem(x + o, X), y, c) for o in range(1, X)]
    peers += [{"chan": lax.rem(z + k, Z)} for k in range(1, Z)]

    barrier = pltpu.get_barrier_semaphore()
    for p in peers:
        pl.semaphore_signal(barrier, inc=1, device_id=p, device_id_type=MESH)

    cols = lambda h: pl.ds(pl.multiple_of(h * HD, HD), HD)
    in_gi = pltpu.make_async_copy(gi_hbm, gi, s_in.at[0])
    in_vi = pltpu.make_async_copy(vi_hbm, vi, s_in.at[1])
    in_go = pltpu.make_async_copy(go_hbm, go, s_in.at[2])
    in_q = pltpu.make_async_copy(q_hbm.at[:, cols(x)], qb.at[c, x], s_in.at[3])
    in_k = pltpu.make_async_copy(k_hbm.at[:, cols(x)], kb.at[0, x], s_in.at[4])
    in_gi.start()
    in_vi.start()
    in_go.start()
    in_q.start()
    in_k.start()

    def remote(src, dst, sems, n, i, dev):
        return pltpu.make_async_remote_copy(
            src_ref=src,
            dst_ref=dst,
            send_sem=sems.at[i],
            recv_sem=sems.at[n + i],
            device_id=dev,
            device_id_type=MESH,
        )

    rates = pr_ref[...]
    decay = jnp.exp(-rates)
    d_sub = jnp.exp(-float(SUB) * rates)
    wgt = pw_ref[...] * jnp.sqrt(rates)
    chains = T // SUB
    state0 = jnp.zeros(rates.shape, jnp.float32)

    in_gi.wait()
    in_vi.wait()
    g[...] = gi[...].astype(jnp.float32) * vi[...].astype(jnp.float32)

    def scan(emit):
        def body(i, states):
            out = []
            for n in range(chains):
                row = n * SUB + i
                st = decay * states[n] + g[pl.ds(row, 1), :]
                if emit:
                    y0[pl.ds(row, 1), :] = jnp.sum(wgt * st, axis=0, keepdims=True)
                out.append(st)
            return tuple(out)

        return lax.fori_loop(0, SUB, body, (state0,) * chains, unroll=8)

    ends = scan(False)
    total = ends[0]
    for n in range(1, chains):
        total = ends[n] + d_sub * total
    e_own[...] = total

    pl.semaphore_wait(barrier, len(peers))

    e_cp = remote(e_own, e_sib, s_e, 1, 0, sib)
    e_cp.start()

    def x_copy(src, dst, sems, o):
        h = lax.rem(x + o, X)
        return remote(src(h), dst, sems, X, o, seq_id(h, y, c))

    q_cp = [
        x_copy(lambda h: q_hbm.at[:, cols(h)], qb.at[c, x], s_q, o) if o else in_q for o in range(X)
    ]
    k_cp = [
        x_copy(lambda h: k_hbm.at[:, cols(h)], kb.at[0, x], s_kx, o) if o else in_k
        for o in range(X)
    ]
    for o in range(1, X):
        k_cp[o].start()
    for o in range(1, X):
        q_cp[o].start()

    for n in range(Y):
        fp[n] = jnp.exp((-SPAN * n) * rates)
    f_one = jnp.exp(-float(T) * rates)

    e_cp.wait_recv()
    mine, other = e_own[...], e_sib[...]
    first = jnp.where(c == 0, mine, other)
    second = jnp.where(c == 0, other, mine)
    tb[0] = second + f_one * first
    t_cp = [
        remote(tb.at[0], tb.at[k], s_t, Y, k, seq_id(x, lax.rem(y + k, Y), c)) for k in range(1, Y)
    ]
    for k in sorted(range(1, Y), key=lambda k: -min(k, Y - k)):
        t_cp[k - 1].start()

    right = seq_id(x, lax.rem(y + 1, Y), c)
    left = seq_id(x, lax.rem(y + Y - 1, Y), c)

    def offset(i):
        return jnp.where(i < 2, i, X + 1 - i) if X > 2 else i

    def ring(buf, sems, way, d, i):
        piece = lax.rem(x + X - offset(i), X)
        src = d - 1 if way == 0 else (Y - d + 1) % Y
        dst = d if way == 0 else Y - d
        return remote(
            buf.at[src, piece],
            buf.at[dst, piece],
            sems,
            2 * D * X,
            (way * D + d - 1) * X + i,
            right if way == 0 else left,
        )

    def hop(buf, sems, d):
        def one(i, goes):
            for way in (0, 1):
                if d > 1:
                    ring(buf, sems, way, d - 1, i).wait_recv()
                if goes[way]:
                    ring(buf, sems, way, d, i).start()

        if d < D:
            lax.fori_loop(0, X, lambda i, _: (one(i, (True, True)), 0)[1], 0)
        else:
            lax.fori_loop(0, X // 2, lambda i, _: (one(i, (True, False)), 0)[1], 0)
            lax.fori_loop(X // 2, X, lambda i, _: (one(i, (False, True)), 0)[1], 0)

    def enter(buf, sems, copies):
        for i in range(X):
            o = i if (i < 2 or X == 2) else X + 1 - i
            if o:
                copies[o].wait_recv()
            else:
                copies[o].wait()
            for way in (0, 1):
                if D > 1 or (way == 0) == (i < X // 2):
                    ring(buf, sems, way, 1, i).start()

    def last(buf, sems):
        lax.fori_loop(
            0, X // 2, lambda i, _: (ring(buf, sems, 0, D, i).wait_recv(), 0)[1], 0
        )
        lax.fori_loop(
            X // 2, X, lambda i, _: (ring(buf, sems, 1, D, i).wait_recv(), 0)[1], 0
        )

    def drain(buf, sems):
        for d in range(1, D + 1):
            for way in (0, 1):
                lo, hi = (0, X) if d < D else ((0, X // 2) if way == 0 else (X // 2, X))
                lax.fori_loop(
                    lo,
                    hi,
                    lambda i, _, way=way, d=d: (ring(buf, sems, way, d, i).wait_send(), 0)[1],
                    0,
                )

    enter(kb, s_k, k_cp)

    for o in range(X):
        if o:
            q_cp[o].wait_recv()
        else:
            q_cp[o].wait()
    qs_cp = pltpu.make_async_remote_copy(
        src_ref=qb.at[c],
        dst_ref=qb.at[c],
        send_sem=s_q.at[0],
        recv_sem=s_q.at[X],
        device_id=sib,
        device_id_type=MESH,
    )
    qs_cp.start()

    scan(True)
    steps = lax.broadcasted_iota(jnp.int32, (SUB, W), 0).astype(jnp.float32) + 1.0
    for m in range(rates.shape[0]):
        dd[m] = wgt[m : m + 1, :] * jnp.exp(-rates[m : m + 1, :] * steps)

    for k in range(1, Y):
        t_cp[k - 1].wait_recv()
    row_total = fp[Y - 1 - y] * tb[0]
    before = jnp.zeros_like(rates)
    for k in range(1, Y):
        part = tb[k]
        row_total = row_total + fp[Y - 1 - lax.rem(y + Y - k, Y)] * part
        before = before + jnp.where(k <= y, fp[k - 1] * part, 0.0)
    rb[0] = row_total
    r_cp = [
        remote(rb.at[0], rb.at[o], s_r, X, o, seq_id(lax.rem(x + o, X), y, c)) for o in range(1, X)
    ]
    for o in range(1, X):
        r_cp[o - 1].start()

    for d in range(2, min(D, 2) + 1):
        hop(kb, s_k, d)

    for o in range(1, X):
        r_cp[o - 1].wait_recv()
    rows_before = jnp.zeros_like(rates)
    for o in range(1, X):
        fade = jnp.exp((-SPAN * Y * (o - 1)) * rates)
        rows_before = rows_before + jnp.where(o <= x, fade * rb[o], 0.0)
    chip_in = before + fp[y] * rows_before
    carry = jnp.where(c == 0, chip_in, first + f_one * chip_in)

    in_go.wait()
    skip = sg_ref[...]
    for n in range(chains):
        for b in range(SUB // 8):
            r0 = n * SUB + b * 8
            acc = y0[r0 : r0 + 8, :] + skip * g[r0 : r0 + 8, :]
            for m in range(rates.shape[0]):
                acc = acc + dd[m, b * 8 : b * 8 + 8, :] * carry[m : m + 1, :]
            cv[r0 : r0 + 8, :] = go[r0 : r0 + 8, :].astype(jnp.float32) * acc
        carry = ends[n] + d_sub * carry

    squares = jnp.zeros((8, T), jnp.float32)
    for h in range(X):
        block = cv[:, h * HD : (h + 1) * HD].T
        ct[h] = block
        squares = squares + jnp.sum((block * block).reshape(HD // 8, 8, T), axis=0)
    sq[0] = squares
    s_cp = [
        remote(sq.at[0], sq.at[k], s_s, Z, k, {"chan": lax.rem(z + k, Z)}) for k in range(1, Z)
    ]
    for k in sorted(range(1, Z), key=lambda k: -min(k, Z - k)):
        s_cp[k - 1].start()

    to_log2 = math.log2(math.e) / math.sqrt(HD)
    delta = lax.broadcasted_iota(jnp.int32, (T, CORES * T), 0) - lax.broadcasted_iota(
        jnp.int32, (T, CORES * T), 1
    )

    def slot_of(i):
        half = (i + 1) // 2
        return jnp.where(lax.rem(i, 2) == 1, half, lax.rem(Y - half, Y))

    def weigh(j):
        from_y = lax.rem(y + Y - j, Y)
        visible = delta <= (y - from_y) * (CORES * T) - c * T
        for xp in range(X):
            n = (xp + 1) * T
            keys = kb[j, 0 : xp + 1].reshape(n, HD)
            rows = jnp.concatenate([qb[0, xp], qb[1, xp]], axis=0)
            sc = lax.dot_general(
                keys, rows, (((1,), (1,)), ((), ())), preferred_element_type=jnp.float32
            )
            edge = jnp.where(visible, sc[n - T :], NEG)
            top = jnp.max(edge, axis=0, keepdims=True)
            if xp:
                top = jnp.maximum(top, jnp.max(sc[: n - T], axis=0, keepdims=True))
            top = top * to_log2
            ex = jnp.exp2(edge * to_log2 - top)
            tot = jnp.sum(ex, axis=0, keepdims=True)
            pt[j, xp, n - T : n, :] = ex.astype(jnp.bfloat16)
            if xp:
                ex = jnp.exp2(sc[: n - T] * to_log2 - top)
                tot = tot + jnp.sum(ex, axis=0, keepdims=True)
                pt[j, xp, : n - T, :] = ex.astype(jnp.bfloat16)
            ms[j, xp : xp + 1, :] = top
            ls[j, xp : xp + 1, :] = tot

    def weigh_range(a, b):
        lax.fori_loop(a, b, lambda i, _: (weigh(slot_of(i)), 0)[1], 0)

    def mix(j, fresh=False):
        for xp in range(X):
            n = (xp + 1) * T
            vals = jnp.concatenate([vb[j, p] for p in range(xp + 1)], axis=1)
            part = jnp.dot(vals, pt[j, xp, :n, :], preferred_element_type=jnp.float32)
            part = part * ms[j, xp : xp + 1, :]
            for cc in range(CORES):
                piece = part[:, cc * T : (cc + 1) * T]
                if fresh:
                    ac[cc, xp, :HD, :] = piece
                else:
                    ac[cc, xp, :HD, :] += piece

    qs_cp.wait_recv()
    weigh_range(0, 1)
    for d in range(3, min(D, 3) + 1):
        hop(kb, s_k, d)
    ready = min(2 * 1 + 1, Y) if D > 1 else 1
    weigh_range(1, ready)

    for k in range(1, Z):
        s_cp[k - 1].wait_recv()
    squares = sq[0]
    for k in range(1, Z):
        squares = squares + sq[k]
    mean = jnp.sum(squares, axis=0, keepdims=True) / float(W * Z)
    inv = lax.rsqrt(mean + 1e-6)
    for h in range(X):
        vs[h] = (ct[h] * inv).astype(jnp.bfloat16)
    in_v = pltpu.make_async_copy(vs.at[x], vb.at[0, x], s_in.at[5])
    in_v.start()
    v_cp = [x_copy(lambda h: vs.at[h], vb.at[0, x], s_vx, o) if o else in_v for o in range(X)]
    for o in range(1, X):
        v_cp[o].start()
    enter(vb, s_v, v_cp)

    for d in range(4, D + 1):
        hop(kb, s_k, d)
    if D > 2:
        weigh_range(3, 5)
    if D > 2:
        hop(vb, s_v, 2)
    if D > 3:
        weigh_range(5, 7)
    last(kb, s_k)
    weigh_range(Y - 1, Y)

    peak = ms[0]
    for j in range(1, Y):
        peak = jnp.maximum(peak, ms[j])
    tot = jnp.zeros_like(peak)
    for j in range(Y):
        fade = jnp.exp2(ms[j] - peak)
        tot = tot + ls[j] * fade
        ms[j] = fade
    for xp in range(X):
        for cc in range(CORES):
            ac[cc, xp, HD : HD + 1, :] = peak[xp : xp + 1, cc * T : (cc + 1) * T]
            ac[cc, xp, HD + 1 : HD + 2, :] = tot[xp : xp + 1, cc * T : (cc + 1) * T]
            ac[cc, xp, HD + 2 : HD + 8, :] = jnp.zeros((6, T), jnp.float32)

    mix(0, fresh=True)

    def mix_range(a, b):
        lax.fori_loop(a, b, lambda i, _: (mix(slot_of(i)), 0)[1], 0)

    for d in range(2, D + 1):
        if not (d == 2 and D > 2):
            hop(vb, s_v, d)
        if d < D or D == 2:
            pass
        mix_range(2 * d - 3, 2 * d - 1)
    last(vb, s_v)
    mix_range(Y - 1, Y)

    m_cp = [remote(ac.at[1 - c, xp], orx.at[xp], s_m, X, xp, sib) for xp in range(X)]
    for xp in range(X):
        m_cp[xp].start()
    for xp in range(X):
        m_cp[xp].wait_recv()
    out_cp = []
    for o in list(range(1, X)) + [0]:
        xp = lax.rem(x + o, X)
        m0, m1 = ac[c, xp, HD : HD + 1, :], orx[xp, HD : HD + 1, :]
        l0, l1 = ac[c, xp, HD + 1 : HD + 2, :], orx[xp, HD + 1 : HD + 2, :]
        top = jnp.maximum(m0, m1)
        a0, a1 = jnp.exp2(m0 - top), jnp.exp2(m1 - top)
        both = (ac[c, xp, :HD, :] * a0 + orx[xp, :HD, :] * a1) / (l0 * a0 + l1 * a1)
        fs[o] = both.T.astype(jnp.bfloat16)
        if o:
            cp = remote(fs.at[o], o_ref.at[:, cols(x)], s_o, X, o, seq_id(xp, y, c))
        else:
            cp = pltpu.make_async_copy(fs.at[0], o_ref.at[:, cols(x)], s_in.at[6])
        cp.start()
        out_cp.append(cp)

    e_cp.wait_send()
    qs_cp.wait_send()
    for o in range(1, X):
        q_cp[o].wait_send()
        k_cp[o].wait_send()
        v_cp[o].wait_send()
        r_cp[o - 1].wait_send()
    for cp in t_cp + s_cp + m_cp:
        cp.wait_send()
    drain(kb, s_k)
    drain(vb, s_v)
    for cp in out_cp:
        cp.wait()


def local(X, Y, Z, go, gi, vi, pr, pw, sg, q, k):
    T, W = go.shape
    modes = pr.shape[0]
    D = Y // 2
    f32, bf16 = jnp.float32, jnp.bfloat16
    hbm = pl.BlockSpec(memory_space=pl.ANY)
    vmem = pl.BlockSpec(memory_space=pltpu.VMEM)
    dma = lambda n: pltpu.SemaphoreType.DMA((n,))
    return pl.pallas_call(
        functools.partial(kernel, X, Y, Z),
        out_shape=jax.ShapeDtypeStruct((T, W), bf16),
        in_specs=[hbm, hbm, hbm, vmem, vmem, vmem, hbm, hbm],
        out_specs=vmem,
        scratch_shapes=[
            pltpu.VMEM((T, W), bf16),
            pltpu.VMEM((T, W), bf16),
            pltpu.VMEM((T, W), bf16),
            pltpu.VMEM((T, W), f32),
            pltpu.VMEM((T, W), f32),
            pltpu.VMEM((T, W), f32),
            pltpu.VMEM((X, HD, T), f32),
            pltpu.VMEM((modes, SUB, W), f32),
            pltpu.VMEM((Y, modes, W), f32),
            pltpu.VMEM((modes, W), f32),
            pltpu.VMEM((modes, W), f32),
            pltpu.VMEM((Y, modes, W), f32),
            pltpu.VMEM((X, modes, W), f32),
            pltpu.VMEM((Z, 8, T), f32),
            pltpu.VMEM((X, HD, T), bf16),
            pltpu.VMEM((CORES, X, T, HD), bf16),
            pltpu.VMEM((Y, X, T, HD), bf16),
            pltpu.VMEM((Y, X, HD, T), bf16),
            pltpu.VMEM((Y, X, X * T, CORES * T), bf16),
            pltpu.VMEM((Y, X, CORES * T), f32),
            pltpu.VMEM((Y, X, CORES * T), f32),
            pltpu.VMEM((CORES, X, HD + 8, T), f32),
            pltpu.VMEM((X, HD + 8, T), f32),
            pltpu.VMEM((X, T, HD), bf16),
            dma(8),
            dma(2),
            dma(2 * Y),
            dma(2 * X),
            dma(2 * Z),
            dma(2 * X),
            dma(2 * X),
            dma(4 * D * X),
            dma(2 * X),
            dma(4 * D * X),
            dma(2 * X),
            dma(2 * X),
        ],
        compiler_params=pltpu.CompilerParams(
            collective_id=0, has_side_effects=True, vmem_limit_bytes=48 * 1024 * 1024
        ),
    )(go, gi, vi, pr, pw, sg.reshape(1, W), q, k)


def solution(mesh, X=4, Y=8):
    Z = mesh.shape["chan"]
    rows = P("seq", "chan")
    in_specs = (rows, rows, rows, P(None, "chan"), P(None, "chan"), P("chan"), rows, rows)
    return jax.shard_map(
        functools.partial(local, X, Y, Z),
        mesh=mesh,
        in_specs=in_specs,
        out_specs=rows,
        check_vma=False,
    )
```

time: 433 us -> 62.5 us (0.14); the launches traced: 427 us -> 62.1 us
  waiting for transfers between devices: 205 us -> 0 us
  blocking collectives: 146 us -> 0 us
  Pallas kernels: 0 us -> 54.8 us
  local copies, waits for them, and re-layouts: 33.7 us -> 7.29 us
  other arithmetic: 14.1 us -> 0 us
  matrix products: 13.9 us -> 0 us
  between operations: 13.3 us -> 0.02 us
    all_gather x3 -> x0, waiting for transfers between devices: 205 us -> none  [the longest x1 183 us: local(): lax.all_gather(values, 'seq', axis=0, tiled=True)]
    unnamed x1 -> x0, blocking collectives: 130 us -> none
    pallas_call x0 -> x1, Pallas kernels: none -> 54.8 us  [local(): pl.pallas_call(functools.partial(kernel, X, Y, Z), out_shape=jax.ShapeDty...]
    dynamic_slice x24 -> x0, local copies, waits for them, and re-layouts: 25.1 us -> none  [the longest x16 14.7 us: one_step(): value_part = lax.dynamic_slice_in_dim(value_piece, sub_start, step_rows, 0)]
    psum x1 -> x0, blocking collectives: 16 us -> none  [local(): total_squares = lax.psum(local_squares, 'chan')]
    dot_general x17 -> x0, matrix products: 13.9 us -> none  [the longest x8 7.32 us: block_update(): jnp.einsum('hqk,khd->hqd', expo.astype(jnp.bfloat16), value_heads, prefer...]
    reduce_sum x10 -> x0, other arithmetic: 7 us -> none  [the longest x8 4.27 us: block_update(): new_sum = run_sum * rescale + jnp.sum(expo, axis=2)]
  transfers between devices with their start and end apart: 3 -> 0, of which waited for: 2 -> 0; matrix products, arithmetic and copies ran while one was open for 3% -> 0% of each run, Pallas kernels for 0% -> 0%
where the time goes in v1:
time: 62.5 us; the launch traced here: 62.1 us
  Pallas kernels  54.8 us (88%)
  local copies, waits for them, and re-layouts  7.29 us (12%)
    pallas_call x1, Pallas kernels, local(): pl.pallas_call(functools.partial(kernel, X, Y, Z), out_shape=jax.ShapeDty...  54.8 us
    unnamed x17, local copies, waits for them, and re-layouts  7.29 us

profile of v1, /device:TPU:1, one launch (start us, length us, event | category | flops | bytes accessed | tf_op | source)
XLA Modules:
  0.0 62.1 jit_solution(15907612793203988193)
XLA Ops:
  0.0 0.0 copy-start
  0.0 0.9 %copy-done = bf16[128,512]{1,0:T(8,128)(2,1)S(1)} copy-done((bf16[128,512]{1,0:T(8,128)(2,1)S(1)}, bf16[128,512]{1,0:T(8,128)(2,1)}, u32[]{:S(2)}) %copy-start) | copy-done | bytes 131096
  0.9 0.0 copy-start.1
  0.9 0.9 %copy-done.1 = bf16[128,512]{1,0:T(8,128)(2,1)S(1)} copy-done((bf16[128,512]{1,0:T(8,128)(2,1)S(1)}, bf16[128,512]{1,0:T(8,128)(2,1)}, u32[]{:S(2)}) %copy-start.1) | copy-done | bytes 131096
  1.8 0.0 copy-start.2
  1.8 0.9 %copy-done.2 = bf16[128,512]{1,0:T(8,128)(2,1)S(1)} copy-done((bf16[128,512]{1,0:T(8,128)(2,1)S(1)}, bf16[128,512]{1,0:T(8,128)(2,1)}, u32[]{:S(2)}) %copy-start.2) | copy-done | bytes 131096
  2.7 0.0 copy-start.3
  2.7 0.9 %copy-done.3 = bf16[128,512]{1,0:T(8,128)(2,1)S(1)} copy-done((bf16[128,512]{1,0:T(8,128)(2,1)S(1)}, bf16[128,512]{1,0:T(8,128)(2,1)}, u32[]{:S(2)}) %copy-start.3) | copy-done | bytes 131096
  3.6 0.0 copy-start.4
  3.6 0.9 %copy-done.4 = bf16[128,512]{1,0:T(8,128)(2,1)S(1)} copy-done((bf16[128,512]{1,0:T(8,128)(2,1)S(1)}, bf16[128,512]{1,0:T(8,128)(2,1)}, u32[]{:S(2)}) %copy-start.4) | copy-done | bytes 131096
  4.5 0.0 copy-start.5
  4.5 0.7 %copy-done.5 = f32[8,512]{1,0:T(8,128)S(1)} copy-done((f32[8,512]{1,0:T(8,128)S(1)}, f32[8,512]{1,0:T(8,128)}, u32[]{:S(2)}) %copy-start.5) | copy-done | bytes 16408
  5.2 0.0 copy-start.6
  5.2 0.7 %copy-done.6 = f32[8,512]{1,0:T(8,128)S(1)} copy-done((f32[8,512]{1,0:T(8,128)S(1)}, f32[8,512]{1,0:T(8,128)}, u32[]{:S(2)}) %copy-start.6) | copy-done | bytes 16408
  6.0 0.0 copy-start.7
  6.0 0.7 %copy-done.7 = f32[512]{0:T(512)S(1)} copy-done((f32[512]{0:T(512)S(1)}, f32[512]{0:T(512)}, u32[]{:S(2)}) %copy-start.7) | copy-done | bytes 2072
  6.6 54.8 %shard_map.82 = bf16[128,512]{1,0:T(8,128)(2,1)S(1)} custom-call(bf16[128,512]{1,0:T(8,128)(2,1)S(1)} %copy-done, bf16[128,512]{1,0:T(8,128)(2,1)S(1)} %copy-done.1, bf16[128,512]{1,0:T(8,128)(2,1)S(1)} %copy-done.2, f32[8,512]{1,0:T(8,128)S(1)} %copy-done.5, f32[8,512]{1,0:T(8,128)S(1)} %copy-done.6, f32[1,512]{1,0:T(1,128)S(1)} %bitcast.1, ...), custom_call_target="tpu_custom_call" | custom-call | tf_op jit(solution)/shard_map/pallas_call | solution.py:471
  61.5 0.7 %copy.10 = bf16[128,512]{1,0:T(8,128)(2,1)} copy(bf16[128,512]{1,0:T(8,128)(2,1)S(1)} %shard_map.82) | data formatting | bytes 262144
Async XLA Ops:
  0.0 0.9 %copy-start = (bf16[128,512]{1,0:T(8,128)(2,1)S(1)}, bf16[128,512]{1,0:T(8,128)(2,1)}, u32[]{:S(2)}) copy-start(bf16[128,512]{1,0:T(8,128)(2,1)} %go_hbm.1) | copy-start | bytes 393220
  0.9 0.9 %copy-start.1 = (bf16[128,512]{1,0:T(8,128)(2,1)S(1)}, bf16[128,512]{1,0:T(8,128)(2,1)}, u32[]{:S(2)}) copy-start(bf16[128,512]{1,0:T(8,128)(2,1)} %gi_hbm.1) | copy-start | bytes 393220
  1.8 0.9 %copy-start.2 = (bf16[128,512]{1,0:T(8,128)(2,1)S(1)}, bf16[128,512]{1,0:T(8,128)(2,1)}, u32[]{:S(2)}) copy-start(bf16[128,512]{1,0:T(8,128)(2,1)} %vi_hbm.1) | copy-start | bytes 393220
  2.7 0.9 %copy-start.3 = (bf16[128,512]{1,0:T(8,128)(2,1)S(1)}, bf16[128,512]{1,0:T(8,128)(2,1)}, u32[]{:S(2)}) copy-start(bf16[128,512]{1,0:T(8,128)(2,1)} %q_hbm.1) | copy-start | bytes 393220
  3.6 0.9 %copy-start.4 = (bf16[128,512]{1,0:T(8,128)(2,1)S(1)}, bf16[128,512]{1,0:T(8,128)(2,1)}, u32[]{:S(2)}) copy-start(bf16[128,512]{1,0:T(8,128)(2,1)} %k_hbm.1) | copy-start | bytes 393220
  4.5 0.7 %copy-start.5 = (f32[8,512]{1,0:T(8,128)S(1)}, f32[8,512]{1,0:T(8,128)}, u32[]{:S(2)}) copy-start(f32[8,512]{1,0:T(8,128)} %pr_ref.1) | copy-start | bytes 49156
  5.2 0.7 %copy-start.6 = (f32[8,512]{1,0:T(8,128)S(1)}, f32[8,512]{1,0:T(8,128)}, u32[]{:S(2)}) copy-start(f32[8,512]{1,0:T(8,128)} %pw_ref.1) | copy-start | bytes 49156
  6.0 0.7 %copy-start.7 = (f32[512]{0:T(512)S(1)}, f32[512]{0:T(512)}, u32[]{:S(2)}) copy-start(f32[512]{0:T(512)} %param.13) | copy-start | bytes 6148

commit v2 on v1

--- a/solution.py
+++ b/solution.py
@@ -22,19 +22,21 @@
     go_hbm,
     gi_hbm,
     vi_hbm,
+    pr_hbm,
+    pw_hbm,
+    sg_hbm,
+    q_hbm,
+    k_hbm,
+    o_ref,
     pr_ref,
     pw_ref,
     sg_ref,
-    q_hbm,
-    k_hbm,
-    o_ref,
     go,
     gi,
     vi,
     g,
     y0,
     cv,
-    ct,
     dd,
     fp,
     e_own,
@@ -42,6 +44,7 @@
     tb,
     rb,
     sq,
+    rr,
     vs,
     qb,
     kb,
@@ -57,6 +60,8 @@
     s_t,
     s_r,
     s_s,
+    s_rx,
+    s_ry,
     s_q,
     s_kx,
     s_k,
@@ -95,8 +100,14 @@
     in_go = pltpu.make_async_copy(go_hbm, go, s_in.at[2])
     in_q = pltpu.make_async_copy(q_hbm.at[:, cols(x)], qb.at[c, x], s_in.at[3])
     in_k = pltpu.make_async_copy(k_hbm.at[:, cols(x)], kb.at[0, x], s_in.at[4])
+    in_pr = pltpu.make_async_copy(pr_hbm, pr_ref, s_in.at[7])
+    in_pw = pltpu.make_async_copy(pw_hbm, pw_ref, s_in.at[8])
+    in_sg = pltpu.make_async_copy(sg_hbm, sg_ref, s_in.at[9])
     in_gi.start()
     in_vi.start()
+    in_pr.start()
+    in_pw.start()
+    in_sg.start()
     in_go.start()
     in_q.start()
     in_k.start()
@@ -111,6 +122,8 @@
             device_id_type=MESH,
         )
 
+    in_pr.wait()
+    in_pw.wait()
     rates = pr_ref[...]
     decay = jnp.exp(-rates)
     d_sub = jnp.exp(-float(SUB) * rates)
@@ -139,12 +152,16 @@
     total = ends[0]
     for n in range(1, chains):
         total = ends[n] + d_sub * total
-    e_own[...] = total
+    f_one = jnp.exp(-float(T) * rates)
+    tb[0] = jnp.where(c == 0, f_one * total, total)
 
     pl.semaphore_wait(barrier, len(peers))
 
-    e_cp = remote(e_own, e_sib, s_e, 1, 0, sib)
-    e_cp.start()
+    t_cp = [
+        remote(tb.at[0], tb.at[k], s_t, Y, k, seq_id(x, lax.rem(y + k, Y), c)) for k in range(1, Y)
+    ]
+    for k in sorted(range(1, Y), key=lambda k: -min(k, Y - k)):
+        t_cp[k - 1].start()
 
     def x_copy(src, dst, sems, o):
         h = lax.rem(x + o, X)
@@ -161,21 +178,6 @@
         k_cp[o].start()
     for o in range(1, X):
         q_cp[o].start()
-
-    for n in range(Y):
-        fp[n] = jnp.exp((-SPAN * n) * rates)
-    f_one = jnp.exp(-float(T) * rates)
-
-    e_cp.wait_recv()
-    mine, other = e_own[...], e_sib[...]
-    first = jnp.where(c == 0, mine, other)
-    second = jnp.where(c == 0, other, mine)
-    tb[0] = second + f_one * first
-    t_cp = [
-        remote(tb.at[0], tb.at[k], s_t, Y, k, seq_id(x, lax.rem(y + k, Y), c)) for k in range(1, Y)
-    ]
-    for k in sorted(range(1, Y), key=lambda k: -min(k, Y - k)):
-        t_cp[k - 1].start()
 
     right = seq_id(x, lax.rem(y + 1, Y), c)
     left = seq_id(x, lax.rem(y + Y - 1, Y), c)
@@ -210,8 +212,8 @@
             lax.fori_loop(0, X // 2, lambda i, _: (one(i, (True, False)), 0)[1], 0)
             lax.fori_loop(X // 2, X, lambda i, _: (one(i, (False, True)), 0)[1], 0)
 
-    def enter(buf, sems, copies):
-        for i in range(X):
+    def enter(buf, sems, copies, lo, hi):
+        for i in range(lo, hi):
             o = i if (i < 2 or X == 2) else X + 1 - i
             if o:
                 copies[o].wait_recv()
@@ -240,7 +242,31 @@
                     0,
                 )
 
-    enter(kb, s_k, k_cp)
+    enter(kb, s_k, k_cp, 0, 1)
+
+    scan(True)
+    for n in range(Y):
+        fp[n] = jnp.exp((-SPAN * n) * rates)
+    steps = lax.broadcasted_iota(jnp.int32, (SUB, W), 0).astype(jnp.float32) + 1.0
+    for m in range(rates.shape[0]):
+        dd[m] = wgt[m : m + 1, :] * jnp.exp(-rates[m : m + 1, :] * steps)
+
+    enter(kb, s_k, k_cp, 1, X)
+
+    for k in range(1, Y):
+        t_cp[k - 1].wait_recv()
+    row_total = fp[Y - 1 - y] * tb[0]
+    before = jnp.zeros_like(rates)
+    for k in range(1, Y):
+        part = tb[k]
+        row_total = row_total + fp[Y - 1 - lax.rem(y + Y - k, Y)] * part
+        before = before + jnp.where(k <= y, fp[k - 1] * part, 0.0)
+    rb[0] = row_total
+    r_cp = [
+        remote(rb.at[0], rb.at[o], s_r, X, o, seq_id(lax.rem(x + o, X), y, c)) for o in range(1, X)
+    ]
+    for o in range(1, X):
+        r_cp[o - 1].start()
 
     for o in range(X):
         if o:
@@ -256,27 +282,6 @@
         device_id_type=MESH,
     )
     qs_cp.start()
-
-    scan(True)
-    steps = lax.broadcasted_iota(jnp.int32, (SUB, W), 0).astype(jnp.float32) + 1.0
-    for m in range(rates.shape[0]):
-        dd[m] = wgt[m : m + 1, :] * jnp.exp(-rates[m : m + 1, :] * steps)
-
-    for k in range(1, Y):
-        t_cp[k - 1].wait_recv()
-    row_total = fp[Y - 1 - y] * tb[0]
-    before = jnp.zeros_like(rates)
-    for k in range(1, Y):
-        part = tb[k]
-        row_total = row_total + fp[Y - 1 - lax.rem(y + Y - k, Y)] * part
-        before = before + jnp.where(k <= y, fp[k - 1] * part, 0.0)
-    rb[0] = row_total
-    r_cp = [
-        remote(rb.at[0], rb.at[o], s_r, X, o, seq_id(lax.rem(x + o, X), y, c)) for o in range(1, X)
-    ]
-    for o in range(1, X):
-        r_cp[o - 1].start()
-
     for d in range(2, min(D, 2) + 1):
         hop(kb, s_k, d)
 
@@ -286,10 +291,15 @@
     for o in range(1, X):
         fade = jnp.exp((-SPAN * Y * (o - 1)) * rates)
         rows_before = rows_before + jnp.where(o <= x, fade * rb[o], 0.0)
-    chip_in = before + fp[y] * rows_before
-    carry = jnp.where(c == 0, chip_in, first + f_one * chip_in)
+    part = before + fp[y] * rows_before
+    e_own[...] = jnp.where(c == 0, f_one * part + total, part)
+    e_cp = remote(e_own, e_sib, s_e, 1, 0, sib)
+    e_cp.start()
+    e_cp.wait_recv()
+    carry = e_sib[...] + jnp.where(c == 0, part, f_one * part)
 
     in_go.wait()
+    in_sg.wait()
     skip = sg_ref[...]
     for n in range(chains):
         for b in range(SUB // 8):
@@ -303,14 +313,20 @@
     squares = jnp.zeros((8, T), jnp.float32)
     for h in range(X):
         block = cv[:, h * HD : (h + 1) * HD].T
-        ct[h] = block
+        vs[h] = block.astype(jnp.bfloat16)
         squares = squares + jnp.sum((block * block).reshape(HD // 8, 8, T), axis=0)
-    sq[0] = squares
+    in_v = pltpu.make_async_copy(vs.at[x], vb.at[0, x], s_in.at[5])
+    in_v.start()
+    v_cp = [x_copy(lambda h: vs.at[h], vb.at[0, x], s_vx, o) if o else in_v for o in range(X)]
+    for o in range(1, X):
+        v_cp[o].start()
+    sq[0] = jnp.sum(squares, axis=0, keepdims=True)
     s_cp = [
         remote(sq.at[0], sq.at[k], s_s, Z, k, {"chan": lax.rem(z + k, Z)}) for k in range(1, Z)
     ]
     for k in sorted(range(1, Z), key=lambda k: -min(k, Z - k)):
         s_cp[k - 1].start()
+    enter(vb, s_v, v_cp, 0, 1)
 
     to_log2 = math.log2(math.e) / math.sqrt(HD)
     delta = lax.broadcasted_iota(jnp.int32, (T, CORES * T), 0) - lax.broadcasted_iota(
@@ -349,10 +365,14 @@
     def weigh_range(a, b):
         lax.fori_loop(a, b, lambda i, _: (weigh(slot_of(i)), 0)[1], 0)
 
-    def mix(j, fresh=False):
-        for xp in range(X):
+    def mix(j, fresh=False, only=None):
+        inv = [rr[j, p] for p in range(X)]
+        for xp in range(X) if only is None else (only,):
             n = (xp + 1) * T
-            vals = jnp.concatenate([vb[j, p] for p in range(xp + 1)], axis=1)
+            vals = [
+                (vb[j, p].astype(jnp.float32) * inv[p]).astype(jnp.bfloat16) for p in range(xp + 1)
+            ]
+            vals = jnp.concatenate(vals, axis=1)
             part = jnp.dot(vals, pt[j, xp, :n, :], preferred_element_type=jnp.float32)
             part = part * ms[j, xp : xp + 1, :]
             for cc in range(CORES):
@@ -362,33 +382,37 @@
                 else:
                     ac[cc, xp, :HD, :] += piece
 
+    def ry(k):
+        return remote(rr.at[0], rr.at[k], s_ry, Y, k, seq_id(x, lax.rem(y + k, Y), c))
+
     qs_cp.wait_recv()
     weigh_range(0, 1)
     for d in range(3, min(D, 3) + 1):
         hop(kb, s_k, d)
-    ready = min(2 * 1 + 1, Y) if D > 1 else 1
-    weigh_range(1, ready)
+    weigh_range(1, 3)
+    enter(vb, s_v, v_cp, 1, X)
 
     for k in range(1, Z):
         s_cp[k - 1].wait_recv()
     squares = sq[0]
     for k in range(1, Z):
         squares = squares + sq[k]
-    mean = jnp.sum(squares, axis=0, keepdims=True) / float(W * Z)
-    inv = lax.rsqrt(mean + 1e-6)
-    for h in range(X):
-        vs[h] = (ct[h] * inv).astype(jnp.bfloat16)
-    in_v = pltpu.make_async_copy(vs.at[x], vb.at[0, x], s_in.at[5])
-    in_v.start()
-    v_cp = [x_copy(lambda h: vs.at[h], vb.at[0, x], s_vx, o) if o else in_v for o in range(X)]
-    for o in range(1, X):
-        v_cp[o].start()
-    enter(vb, s_v, v_cp)
+    rr[0, x] = lax.rsqrt(squares / float(W * Z) + 1e-6)
+    rx_cp = [
+        remote(rr.at[0, x], rr.at[0, x], s_rx, X, o, seq_id(lax.rem(x + o, X), y, c))
+        for o in range(1, X)
+    ]
+    for cp in rx_cp:
+        cp.start()
 
     for d in range(4, D + 1):
         hop(kb, s_k, d)
     if D > 2:
         weigh_range(3, 5)
+    for cp in rx_cp:
+        cp.wait_recv()
+    for k in sorted(range(1, Y), key=lambda k: -min(k, Y - k)):
+        ry(k).start()
     if D > 2:
         hop(vb, s_v, 2)
     if D > 3:
@@ -410,28 +434,36 @@
             ac[cc, xp, HD + 1 : HD + 2, :] = tot[xp : xp + 1, cc * T : (cc + 1) * T]
             ac[cc, xp, HD + 2 : HD + 8, :] = jnp.zeros((6, T), jnp.float32)
 
+    if D > 3:
+        hop(vb, s_v, 3)
     mix(0, fresh=True)
 
     def mix_range(a, b):
-        lax.fori_loop(a, b, lambda i, _: (mix(slot_of(i)), 0)[1], 0)
+        def body(i, _):
+            j = slot_of(i)
+            ry(j).wait_recv()
+            mix(j)
+            return 0
+
+        lax.fori_loop(a, b, body, 0)
 
     for d in range(2, D + 1):
-        if not (d == 2 and D > 2):
+        if not ((d == 2 and D > 2) or (d == 3 and D > 3)):
             hop(vb, s_v, d)
-        if d < D or D == 2:
-            pass
         mix_range(2 * d - 3, 2 * d - 1)
+
+    def merge(xp):
+        return remote(ac.at[1 - c, xp], orx.at[xp], s_m, X, xp, sib)
+
     last(vb, s_v)
-    mix_range(Y - 1, Y)
-
-    m_cp = [remote(ac.at[1 - c, xp], orx.at[xp], s_m, X, xp, sib) for xp in range(X)]
-    for xp in range(X):
-        m_cp[xp].start()
-    for xp in range(X):
-        m_cp[xp].wait_recv()
+    ry(D).wait_recv()
+    for xp in reversed(range(X)):
+        mix(D, only=xp)
+        merge(xp).start()
     out_cp = []
-    for o in list(range(1, X)) + [0]:
+    for o in sorted(range(1, X), key=lambda o: -min(o, X - o)) + [0]:
         xp = lax.rem(x + o, X)
+        merge(xp).wait_recv()
         m0, m1 = ac[c, xp, HD : HD + 1, :], orx[xp, HD : HD + 1, :]
         l0, l1 = ac[c, xp, HD + 1 : HD + 2, :], orx[xp, HD + 1 : HD + 2, :]
         top = jnp.maximum(m0, m1)
@@ -452,8 +484,12 @@
         k_cp[o].wait_send()
         v_cp[o].wait_send()
         r_cp[o - 1].wait_send()
-    for cp in t_cp + s_cp + m_cp:
+    for cp in t_cp + s_cp + rx_cp:
         cp.wait_send()
+    for xp in range(X):
+        merge(xp).wait_send()
+    for k in range(1, Y):
+        ry(k).wait_send()
     drain(kb, s_k)
     drain(vb, s_v)
     for cp in out_cp:
@@ -471,23 +507,26 @@
     return pl.pallas_call(
         functools.partial(kernel, X, Y, Z),
         out_shape=jax.ShapeDtypeStruct((T, W), bf16),
-        in_specs=[hbm, hbm, hbm, vmem, vmem, vmem, hbm, hbm],
+        in_specs=[hbm] * 8,
         out_specs=vmem,
         scratch_shapes=[
+            pltpu.VMEM((modes, W), f32),
+            pltpu.VMEM((modes, W), f32),
+            pltpu.VMEM((1, W), f32),
             pltpu.VMEM((T, W), bf16),
             pltpu.VMEM((T, W), bf16),
             pltpu.VMEM((T, W), bf16),
             pltpu.VMEM((T, W), f32),
             pltpu.VMEM((T, W), f32),
             pltpu.VMEM((T, W), f32),
-            pltpu.VMEM((X, HD, T), f32),
             pltpu.VMEM((modes, SUB, W), f32),
             pltpu.VMEM((Y, modes, W), f32),
             pltpu.VMEM((modes, W), f32),
             pltpu.VMEM((modes, W), f32),
             pltpu.VMEM((Y, modes, W), f32),
             pltpu.VMEM((X, modes, W), f32),
-            pltpu.VMEM((Z, 8, T), f32),
+            pltpu.VMEM((Z, 1, T), f32),
+            pltpu.VMEM((Y, X, 1, T), f32),
             pltpu.VMEM((X, HD, T), bf16),
             pltpu.VMEM((CORES, X, T, HD), bf16),
             pltpu.VMEM((Y, X, T, HD), bf16),
@@ -498,12 +537,14 @@
             pltpu.VMEM((CORES, X, HD + 8, T), f32),
             pltpu.VMEM((X, HD + 8, T), f32),
             pltpu.VMEM((X, T, HD), bf16),
-            dma(8),
+            dma(10),
             dma(2),
             dma(2 * Y),
             dma(2 * X),
             dma(2 * Z),
             dma(2 * X),
+            dma(2 * Y),
+            dma(2 * X),
             dma(2 * X),
             dma(4 * D * X),
             dma(2 * X),
@@ -512,7 +553,7 @@
             dma(2 * X),
         ],
         compiler_params=pltpu.CompilerParams(
-            collective_id=0, has_side_effects=True, vmem_limit_bytes=48 * 1024 * 1024
+            collective_id=0, has_side_effects=True, vmem_limit_bytes=67043328
         ),
     )(go, gi, vi, pr, pw, sg.reshape(1, W), q, k)
 

time: 62.5 us -> 54.5 us (0.87)
  local copies, waits for them, and re-layouts: 7.29 us -> 1.57 us
  Pallas kernels: 54.8 us -> 52.8 us
    unnamed x17 -> x1, local copies, waits for them, and re-layouts: 7.29 us -> 1.57 us
    pallas_call x1, Pallas kernels: 54.8 us -> 52.8 us  [local(): pl.pallas_call(functools.partial(kernel, X, Y, Z), out_shape=jax.ShapeDty...]
where the time goes in v2:
time: 54.5 us; the launch traced here: 54.4 us
  Pallas kernels  52.8 us (97%)
  local copies, waits for them, and re-layouts  1.57 us (3%)
    pallas_call x1, Pallas kernels, local(): pl.pallas_call(functools.partial(kernel, X, Y, Z), out_shape=jax.ShapeDty...  52.8 us
    unnamed x1, local copies, waits for them, and re-layouts  1.57 us

profile of v2, /device:TPU:1, one launch (start us, length us, event | category | flops | bytes accessed | tf_op | source)
XLA Modules:
  0.0 54.4 jit_solution(16534781074005841510)
XLA Ops:
  0.0 52.8 %shard_map.82 = bf16[128,512]{1,0:T(8,128)(2,1)} custom-call(bf16[128,512]{1,0:T(8,128)(2,1)} %go_hbm.1, bf16[128,512]{1,0:T(8,128)(2,1)} %gi_hbm.1, bf16[128,512]{1,0:T(8,128)(2,1)} %vi_hbm.1, f32[8,512]{1,0:T(8,128)} %pr_hbm.1, f32[8,512]{1,0:T(8,128)} %pw_hbm.1, f32[1,512]{1,0:T(1,128)} %bitcast.1, bf16[128,512]{1,0:T(8,128)(2,1)} %q_hbm.1, ...), custom_call_target="tpu_custom_call" | custom-call | tf_op jit(solution)/shard_map/pallas_call | solution.py:507
  52.8 1.6 %copy.10 = bf16[128,512]{1,0:T(8,128)(2,1)} copy(bf16[128,512]{1,0:T(8,128)(2,1)} %shard_map.82) | data formatting | bytes 262144

commit v3 on v2

--- a/solution.py
+++ b/solution.py
@@ -60,7 +60,6 @@
     s_t,
     s_r,
     s_s,
-    s_rx,
     s_ry,
     s_q,
     s_kx,
@@ -86,13 +85,10 @@
 
     sib = {"seq": s + 1 - 2 * c}
     peers = [sib]
-    peers += [seq_id(x, lax.rem(y + k, Y), c) for k in range(1, Y)]
-    peers += [seq_id(lax.rem(x + o, X), y, c) for o in range(1, X)]
     peers += [{"chan": lax.rem(z + k, Z)} for k in range(1, Z)]
-
-    barrier = pltpu.get_barrier_semaphore()
-    for p in peers:
-        pl.semaphore_signal(barrier, inc=1, device_id=p, device_id_type=MESH)
+    peers += [
+        seq_id(lax.rem(x + n % X, X), lax.rem(y + n // X, Y), c) for n in range(1, X * Y)
+    ]
 
     cols = lambda h: pl.ds(pl.multiple_of(h * HD, HD), HD)
     in_gi = pltpu.make_async_copy(gi_hbm, gi, s_in.at[0])
@@ -112,6 +108,10 @@
     in_q.start()
     in_k.start()
 
+    barrier = pltpu.get_barrier_semaphore()
+    for p in peers:
+        pl.semaphore_signal(barrier, inc=1, device_id=p, device_id_type=MESH)
+
     def remote(src, dst, sems, n, i, dev):
         return pltpu.make_async_remote_copy(
             src_ref=src,
@@ -170,15 +170,6 @@
     q_cp = [
         x_copy(lambda h: q_hbm.at[:, cols(h)], qb.at[c, x], s_q, o) if o else in_q for o in range(X)
     ]
-    k_cp = [
-        x_copy(lambda h: k_hbm.at[:, cols(h)], kb.at[0, x], s_kx, o) if o else in_k
-        for o in range(X)
-    ]
-    for o in range(1, X):
-        k_cp[o].start()
-    for o in range(1, X):
-        q_cp[o].start()
-
     right = seq_id(x, lax.rem(y + 1, Y), c)
     left = seq_id(x, lax.rem(y + Y - 1, Y), c)
 
@@ -187,62 +178,100 @@
 
     def ring(buf, sems, way, d, i):
         piece = lax.rem(x + X - offset(i), X)
-        src = d - 1 if way == 0 else (Y - d + 1) % Y
-        dst = d if way == 0 else Y - d
+        start = min(d - 1, 2)
+        far = d - start
+        if way == 0:
+            src, dst, to = start, d, lax.rem(y + far, Y)
+        else:
+            src, dst, to = (Y - start) % Y, Y - d, lax.rem(y + Y - far, Y)
         return remote(
             buf.at[src, piece],
             buf.at[dst, piece],
             sems,
             2 * D * X,
             (way * D + d - 1) * X + i,
-            right if way == 0 else left,
+            seq_id(x, to, c),
         )
 
-    def hop(buf, sems, d):
+    def span(way, d):
+        if d < D:
+            return 0, X
+        return (0, X // 2) if way == 0 else (X // 2, X)
+
+    def each(d, act):
+        for way in (0, 1):
+            lax.fori_loop(*span(way, d), lambda i, _, way=way: (act(way, i), 0)[1], 0)
+
+    def hop(buf, sems, d, lo=0, hi=X):
         def one(i, goes):
             for way in (0, 1):
-                if d > 1:
-                    ring(buf, sems, way, d - 1, i).wait_recv()
-                if goes[way]:
-                    ring(buf, sems, way, d, i).start()
-
-        if d < D:
-            lax.fori_loop(0, X, lambda i, _: (one(i, (True, True)), 0)[1], 0)
-        else:
-            lax.fori_loop(0, X // 2, lambda i, _: (one(i, (True, False)), 0)[1], 0)
-            lax.fori_loop(X // 2, X, lambda i, _: (one(i, (False, True)), 0)[1], 0)
-
-    def enter(buf, sems, copies, lo, hi):
+                ring(buf, sems, way, d - 1, i).wait_recv()
+                for to in (4, 3) if d == 3 else (d,):
+                    if to < D or (to == D and goes[way]):
+                        ring(buf, sems, way, to, i).start()
+
+        for a, b, goes in ((0, X // 2, (True, False)), (X // 2, X, (False, True))):
+            a, b = max(a, lo), min(b, hi)
+            if a < b and d <= D:
+                lax.fori_loop(a, b, lambda i, _, goes=goes: (one(i, goes), 0)[1], 0)
+
+    def got(buf, sems, d):
+        each(d, lambda way, i: ring(buf, sems, way, d, i).wait_recv())
+
+    def drain(buf, sems):
+        for d in range(1, D + 1):
+            each(d, lambda way, i, d=d: ring(buf, sems, way, d, i).wait_send())
+
+    def inject(src, own, buf, sx, sems):
+        far = sorted(range(1, X), key=lambda o: -min(o, X - o))
+        copies = [own]
+
+        def beside(o):
+            i = o if (o < 2 or X == 2) else X + 1 - o
+            h = lax.rem(x + o, X)
+            for way, step, slot in ((0, 1, 1), (1, Y - 1, Y - 1)):
+                cp = remote(
+                    src(h),
+                    buf.at[slot, x],
+                    sems,
+                    2 * D * X,
+                    way * D * X + i,
+                    seq_id(h, lax.rem(y + step, Y), c),
+                )
+                cp.start()
+
+        for o in [0] + far:
+            beside(o)
+        for o in range(1, X):
+            copies.append(x_copy(src, buf.at[0, x], sx, o))
+        for o in far:
+            copies[o].start()
+        return copies
+
+    def entered(copies):
+        copies[0].wait()
+        for cp in copies[1:]:
+            cp.wait_recv()
+
+    k_cp = [in_k] + [
+        x_copy(lambda h: k_hbm.at[:, cols(h)], kb.at[0, x], s_kx, o) for o in range(1, X)
+    ]
+    for o in range(1, X):
+        k_cp[o].start()
+
+    def enter(lo, hi):
         for i in range(lo, hi):
             o = i if (i < 2 or X == 2) else X + 1 - i
             if o:
-                copies[o].wait_recv()
+                k_cp[o].wait_recv()
             else:
-                copies[o].wait()
+                k_cp[o].wait()
             for way in (0, 1):
-                if D > 1 or (way == 0) == (i < X // 2):
-                    ring(buf, sems, way, 1, i).start()
-
-    def last(buf, sems):
-        lax.fori_loop(
-            0, X // 2, lambda i, _: (ring(buf, sems, 0, D, i).wait_recv(), 0)[1], 0
-        )
-        lax.fori_loop(
-            X // 2, X, lambda i, _: (ring(buf, sems, 1, D, i).wait_recv(), 0)[1], 0
-        )
-
-    def drain(buf, sems):
-        for d in range(1, D + 1):
-            for way in (0, 1):
-                lo, hi = (0, X) if d < D else ((0, X // 2) if way == 0 else (X // 2, X))
-                lax.fori_loop(
-                    lo,
-                    hi,
-                    lambda i, _, way=way, d=d: (ring(buf, sems, way, d, i).wait_send(), 0)[1],
-                    0,
-                )
-
-    enter(kb, s_k, k_cp, 0, 1)
+                ring(kb, s_k, way, 1, i).start()
+
+    enter(0, 1)
+    for o in range(1, X):
+        q_cp[o].start()
 
     scan(True)
     for n in range(Y):
@@ -251,7 +280,7 @@
     for m in range(rates.shape[0]):
         dd[m] = wgt[m : m + 1, :] * jnp.exp(-rates[m : m + 1, :] * steps)
 
-    enter(kb, s_k, k_cp, 1, X)
+    enter(1, X)
 
     for k in range(1, Y):
         t_cp[k - 1].wait_recv()
@@ -282,8 +311,7 @@
         device_id_type=MESH,
     )
     qs_cp.start()
-    for d in range(2, min(D, 2) + 1):
-        hop(kb, s_k, d)
+    hop(kb, s_k, 2)
 
     for o in range(1, X):
         r_cp[o - 1].wait_recv()
@@ -317,16 +345,13 @@
         squares = squares + jnp.sum((block * block).reshape(HD // 8, 8, T), axis=0)
     in_v = pltpu.make_async_copy(vs.at[x], vb.at[0, x], s_in.at[5])
     in_v.start()
-    v_cp = [x_copy(lambda h: vs.at[h], vb.at[0, x], s_vx, o) if o else in_v for o in range(X)]
-    for o in range(1, X):
-        v_cp[o].start()
+    v_cp = inject(lambda h: vs.at[h], in_v, vb, s_vx, s_v)
     sq[0] = jnp.sum(squares, axis=0, keepdims=True)
     s_cp = [
         remote(sq.at[0], sq.at[k], s_s, Z, k, {"chan": lax.rem(z + k, Z)}) for k in range(1, Z)
     ]
     for k in sorted(range(1, Z), key=lambda k: -min(k, Z - k)):
         s_cp[k - 1].start()
-    enter(vb, s_v, v_cp, 0, 1)
 
     to_log2 = math.log2(math.e) / math.sqrt(HD)
     delta = lax.broadcasted_iota(jnp.int32, (T, CORES * T), 0) - lax.broadcasted_iota(
@@ -382,15 +407,20 @@
                 else:
                     ac[cc, xp, :HD, :] += piece
 
-    def ry(k):
-        return remote(rr.at[0], rr.at[k], s_ry, Y, k, seq_id(x, lax.rem(y + k, Y), c))
+    def ry(n):
+        dx, dy = lax.rem(n, X), n // X
+        to = seq_id(lax.rem(x + dx, X), lax.rem(y + dy, Y), c)
+        return remote(rr.at[0, x], rr.at[dy, x], s_ry, X * Y, n, to)
+
+    def scales(j, lo=0):
+        for dx in range(lo, X):
+            ry(j * X + dx).wait_recv()
 
     qs_cp.wait_recv()
     weigh_range(0, 1)
-    for d in range(3, min(D, 3) + 1):
-        hop(kb, s_k, d)
+    hop(kb, s_k, 3)
     weigh_range(1, 3)
-    enter(vb, s_v, v_cp, 1, X)
+    hop(vb, s_v, 2, 0, X // 2)
 
     for k in range(1, Z):
         s_cp[k - 1].wait_recv()
@@ -398,27 +428,15 @@
     for k in range(1, Z):
         squares = squares + sq[k]
     rr[0, x] = lax.rsqrt(squares / float(W * Z) + 1e-6)
-    rx_cp = [
-        remote(rr.at[0, x], rr.at[0, x], s_rx, X, o, seq_id(lax.rem(x + o, X), y, c))
-        for o in range(1, X)
-    ]
-    for cp in rx_cp:
-        cp.start()
-
-    for d in range(4, D + 1):
-        hop(kb, s_k, d)
+    lax.fori_loop(1, X * Y, lambda n, _: (ry(n).start(), 0)[1], 0)
+
+    hop(vb, s_v, 2, X // 2, X)
     if D > 2:
         weigh_range(3, 5)
-    for cp in rx_cp:
-        cp.wait_recv()
-    for k in sorted(range(1, Y), key=lambda k: -min(k, Y - k)):
-        ry(k).start()
-    if D > 2:
-        hop(vb, s_v, 2)
-    if D > 3:
-        weigh_range(5, 7)
-    last(kb, s_k)
-    weigh_range(Y - 1, Y)
+        hop(vb, s_v, 3)
+        got(kb, s_k, 3)
+    got(kb, s_k, D)
+    weigh_range(5 if D > 2 else 3, Y)
 
     peak = ms[0]
     for j in range(1, Y):
@@ -434,29 +452,31 @@
             ac[cc, xp, HD + 1 : HD + 2, :] = tot[xp : xp + 1, cc * T : (cc + 1) * T]
             ac[cc, xp, HD + 2 : HD + 8, :] = jnp.zeros((6, T), jnp.float32)
 
-    if D > 3:
-        hop(vb, s_v, 3)
+    entered(v_cp)
+    scales(0, 1)
     mix(0, fresh=True)
 
     def mix_range(a, b):
         def body(i, _):
             j = slot_of(i)
-            ry(j).wait_recv()
+            scales(j)
             mix(j)
             return 0
 
         lax.fori_loop(a, b, body, 0)
 
-    for d in range(2, D + 1):
-        if not ((d == 2 and D > 2) or (d == 3 and D > 3)):
-            hop(vb, s_v, d)
-        mix_range(2 * d - 3, 2 * d - 1)
+    if D > 2:
+        mix_range(1, 5)
+        got(vb, s_v, 3)
+        mix_range(5, 7)
+    else:
+        mix_range(1, 3)
 
     def merge(xp):
         return remote(ac.at[1 - c, xp], orx.at[xp], s_m, X, xp, sib)
 
-    last(vb, s_v)
-    ry(D).wait_recv()
+    got(vb, s_v, D)
+    scales(D)
     for xp in reversed(range(X)):
         mix(D, only=xp)
         merge(xp).start()
@@ -484,12 +504,11 @@
         k_cp[o].wait_send()
         v_cp[o].wait_send()
         r_cp[o - 1].wait_send()
-    for cp in t_cp + s_cp + rx_cp:
+    for cp in t_cp + s_cp:
         cp.wait_send()
     for xp in range(X):
         merge(xp).wait_send()
-    for k in range(1, Y):
-        ry(k).wait_send()
+    lax.fori_loop(1, X * Y, lambda n, _: (ry(n).wait_send(), 0)[1], 0)
     drain(kb, s_k)
     drain(vb, s_v)
     for cp in out_cp:
@@ -542,8 +561,7 @@
             dma(2 * Y),
             dma(2 * X),
             dma(2 * Z),
-            dma(2 * X),
-            dma(2 * Y),
+            dma(2 * X * Y),
             dma(2 * X),
             dma(2 * X),
             dma(4 * D * X),

time: 54.5 us -> 53.7 us (0.985)
  Pallas kernels: 52.8 us -> 51.9 us
    pallas_call x1, Pallas kernels: 52.8 us -> 51.9 us  [local(): pl.pallas_call(functools.partial(kernel, X, Y, Z), out_shape=jax.ShapeDty...]
where the time goes in v3:
time: 53.7 us; the launch traced here: 53.5 us
  Pallas kernels  51.9 us (97%)
  local copies, waits for them, and re-layouts  1.57 us (3%)
    pallas_call x1, Pallas kernels, local(): pl.pallas_call(functools.partial(kernel, X, Y, Z), out_shape=jax.ShapeDty...  51.9 us
    unnamed x1, local copies, waits for them, and re-layouts  1.57 us

profile of v3, /device:TPU:1, one launch (start us, length us, event | category | flops | bytes accessed | tf_op | source)
XLA Modules:
  0.0 53.5 jit_solution(17963870255289271542)
XLA Ops:
  0.0 51.9 %shard_map.82 = bf16[128,512]{1,0:T(8,128)(2,1)} custom-call(bf16[128,512]{1,0:T(8,128)(2,1)} %go_hbm.1, bf16[128,512]{1,0:T(8,128)(2,1)} %gi_hbm.1, bf16[128,512]{1,0:T(8,128)(2,1)} %vi_hbm.1, f32[8,512]{1,0:T(8,128)} %pr_hbm.1, f32[8,512]{1,0:T(8,128)} %pw_hbm.1, f32[1,512]{1,0:T(1,128)} %bitcast.1, bf16[128,512]{1,0:T(8,128)(2,1)} %q_hbm.1, ...), custom_call_target="tpu_custom_call" | custom-call | tf_op jit(solution)/shard_map/pallas_call | solution.py:526
  52.0 1.6 %copy.10 = bf16[128,512]{1,0:T(8,128)(2,1)} copy(bf16[128,512]{1,0:T(8,128)(2,1)} %shard_map.82) | data formatting | bytes 262144

commit v4 on v3

--- a/solution.py
+++ b/solution.py
@@ -178,7 +178,7 @@
 
     def ring(buf, sems, way, d, i):
         piece = lax.rem(x + X - offset(i), X)
-        start = min(d - 1, 2)
+        start = min(d - 1, 2) if buf is vb else d - 1
         far = d - start
         if way == 0:
             src, dst, to = start, d, lax.rem(y + far, Y)
@@ -206,7 +206,7 @@
         def one(i, goes):
             for way in (0, 1):
                 ring(buf, sems, way, d - 1, i).wait_recv()
-                for to in (4, 3) if d == 3 else (d,):
+                for to in (4, 3) if d == 3 and buf is vb else (d,):
                     if to < D or (to == D and goes[way]):
                         ring(buf, sems, way, to, i).start()
 
@@ -421,6 +421,7 @@
     hop(kb, s_k, 3)
     weigh_range(1, 3)
     hop(vb, s_v, 2, 0, X // 2)
+    hop(kb, s_k, 4)
 
     for k in range(1, Z):
         s_cp[k - 1].wait_recv()
@@ -434,7 +435,6 @@
     if D > 2:
         weigh_range(3, 5)
         hop(vb, s_v, 3)
-        got(kb, s_k, 3)
     got(kb, s_k, D)
     weigh_range(5 if D > 2 else 3, Y)
 

time: 53.7 us -> 53.1 us (0.989)
    pallas_call x1, Pallas kernels: 51.9 us -> 51.4 us  [local(): pl.pallas_call(functools.partial(kernel, X, Y, Z), out_shape=jax.ShapeDty...]
where the time goes in v4:
time: 53.1 us; the launch traced here: 52.9 us
  Pallas kernels  51.4 us (97%)
  local copies, waits for them, and re-layouts  1.57 us (3%)
    pallas_call x1, Pallas kernels, local(): pl.pallas_call(functools.partial(kernel, X, Y, Z), out_shape=jax.ShapeDty...  51.4 us
    unnamed x1, local copies, waits for them, and re-layouts  1.57 us

profile of v4, /device:TPU:1, one launch (start us, length us, event | category | flops | bytes accessed | tf_op | source)
XLA Modules:
  0.0 52.9 jit_solution(13670689335068415827)
XLA Ops:
  0.0 51.4 %shard_map.82 = bf16[128,512]{1,0:T(8,128)(2,1)} custom-call(bf16[128,512]{1,0:T(8,128)(2,1)} %go_hbm.1, bf16[128,512]{1,0:T(8,128)(2,1)} %gi_hbm.1, bf16[128,512]{1,0:T(8,128)(2,1)} %vi_hbm.1, f32[8,512]{1,0:T(8,128)} %pr_hbm.1, f32[8,512]{1,0:T(8,128)} %pw_hbm.1, f32[1,512]{1,0:T(1,128)} %bitcast.1, bf16[128,512]{1,0:T(8,128)(2,1)} %q_hbm.1, ...), custom_call_target="tpu_custom_call" | custom-call | tf_op jit(solution)/shard_map/pallas_call | solution.py:526
  51.4 1.6 %copy.10 = bf16[128,512]{1,0:T(8,128)(2,1)} copy(bf16[128,512]{1,0:T(8,128)(2,1)} %shard_map.82) | data formatting | bytes 262144
